TPU v7x, 32 devices: a whole 2x2x4 slice. The times are simulated.
32 devices in a mesh: row: 4 (over y, x), col: 2 (over core), depth: 4 (over z).
Axes of the slice: x: 2, y: 2, z: 4, core: 2. Of those that a mesh axis runs over, the one named last changes fastest.
Arguments:
- source_desc: bfloat16 [2048, 256], P(('row', 'col', 'depth')), may hold values from -4 to 4
- target_desc: bfloat16 [16384, 256], P(('col', 'depth', 'row')), may hold values from -4 to 4
- target_dual: float32 [16384], P(('col', 'depth')), may hold values from -2 to 4.25
- row_weight: float32 [2048], P('row'), may hold values from 0.3 to 3
- matches: int32 [2048], P('row'), may hold values from 0 to 16383
Outputs:
- grad_source: float32 [2048, 256], P(('row', 'col', 'depth'))
- grad_target: float32 [16384, 256], P(('col', 'depth', 'row'))
All inputs are finite; a program needn't handle non-finite values.
Results may differ from a plain program's by a relative error of at most 0.0029.
Values may be sent and summed in bfloat16 or wider, within the bound.
A program may use at most 64 MiB of HBM per device.

v0:
```python
import jax
import jax.numpy as jnp
from jax import lax
from jax.sharding import PartitionSpec as P

PANELS = 2


score_scale = 0.1875


def combined_all(value, axis, join):
    pieces = jax.tree.map(lambda part: lax.all_gather(part, axis), value)
    head = jax.tree.map(lambda part: part[0], pieces)
    tail = jax.tree.map(lambda part: part[1:], pieces)
    so_far, _ = lax.scan(lambda so_far, section: (join(so_far, section), None), head, tail)
    return so_far


def combine_stats(earlier, later):
    highest = jnp.maximum(earlier[0], later[0])
    mass_sum = earlier[1] * jnp.exp(earlier[0] - highest) + later[1] * jnp.exp(later[0] - highest)
    return (highest, mass_sum)


def panel_scores(src_rows, targets, target_dual):
    products = jnp.einsum("id,jd->ij", src_rows, targets, preferred_element_type=jnp.float32)
    return score_scale * products + target_dual[None, :]


def local_stats(scores):
    highest = jnp.max(scores, axis=1)
    mass_sum = jnp.sum(jnp.exp(scores - highest[:, None]), axis=1)
    return (highest, mass_sum)


def panel_delta(scores, highest, mass_sum, weights, wanted, columns):
    log_total = highest + jnp.log(mass_sum)
    plan_tile = jnp.exp(scores - log_total[:, None])
    hit_mask = (columns[None, :] == wanted[:, None]).astype(jnp.float32)
    return (weights[:, None] * (plan_tile - hit_mask)).astype(jnp.bfloat16)


def per_device(source_desc, target_desc, target_dual, row_weight, matches):
    sources = lax.all_gather(source_desc, ("col", "depth"), axis=0, tiled=True)
    targets = lax.all_gather(target_desc, "row", axis=0, tiled=True)
    row_count = sources.shape[0]
    col_count = targets.shape[0]
    height = row_count // PANELS
    offset = (lax.axis_index("col") * lax.axis_size("depth") + lax.axis_index("depth")) * col_count
    columns = offset + lax.iota(jnp.int32, col_count)
    deltas = []
    top_parts = []
    mass_parts = []
    for panel_idx in range(PANELS):
        first_row = panel_idx * height
        last_row = first_row + height
        scores = panel_scores(sources[first_row:last_row], targets, target_dual)
        local_top, local_mass = local_stats(scores)
        highest, mass_sum = combined_all((local_top, local_mass), ("col", "depth"), combine_stats)
        top_parts.append(highest)
        mass_parts.append(mass_sum)
        deltas.append(
            panel_delta(
                scores,
                highest,
                mass_sum,
                row_weight[first_row:last_row],
                matches[first_row:last_row],
                columns,
            )
        )
    all_highest = jnp.concatenate(top_parts, axis=0)
    all_mass = jnp.concatenate(mass_parts, axis=0)
    delta_all = jnp.concatenate(deltas, axis=0)
    grad_source = lax.psum_scatter(
        score_scale * jnp.dot(delta_all, targets, preferred_element_type=jnp.float32),
        ("col", "depth"),
        scatter_dimension=0,
        tiled=True,
    )
    own_count = target_desc.shape[0]
    own_start = lax.axis_index("row") * own_count
    own_dual = lax.dynamic_slice_in_dim(target_dual, own_start, own_count, 0)
    own_columns = offset + own_start + lax.iota(jnp.int32, own_count)
    match_float = matches.astype(jnp.float32)
    every_top, every_mass, every_weight, every_match = (
        lax.all_gather(all_highest, "row", axis=0, tiled=True),
        lax.all_gather(all_mass, "row", axis=0, tiled=True),
        lax.all_gather(row_weight, "row", axis=0, tiled=True),
        lax.all_gather(match_float, "row", axis=0, tiled=True),
    )
    every_wanted = every_match.astype(jnp.int32)

    def block_term(rows_block, first):
        span = rows_block.shape[0]
        tops = lax.dynamic_slice_in_dim(every_top, first, span, 0)
        masses = lax.dynamic_slice_in_dim(every_mass, first, span, 0)
        weights = lax.dynamic_slice_in_dim(every_weight, first, span, 0)
        wanted = lax.dynamic_slice_in_dim(every_wanted, first, span, 0)
        scores = panel_scores(rows_block, target_desc, own_dual)
        delta_block = panel_delta(scores, tops, masses, weights, wanted, own_columns)
        return score_scale * jnp.einsum(
            "ij,id->jd", delta_block, rows_block, preferred_element_type=jnp.float32
        )

    def fold_rows(total, piece, start):
        span = piece.shape[0]
        if span > 2048 and span % 2048 == 0:
            stacked = piece.reshape(span // 2048, 2048, piece.shape[1])

            def step_block(carry, packed):
                block_idx, rows_block = packed
                return (carry + block_term(rows_block, start + block_idx * 2048), None)

            block_ids = lax.iota(jnp.int32, span // 2048)
            total, unused = lax.scan(step_block, total, (block_ids, stacked))
            return total
        return total + block_term(piece, start)

    empty = jnp.zeros((own_count, target_desc.shape[1]), jnp.float32)
    grad_target = fold_rows(empty, lax.all_gather(sources, "row", axis=0, tiled=True), jnp.int32(0))
    return (grad_source, grad_target)


def solution(mesh):
    return jax.shard_map(
        per_device,
        mesh=mesh,
        in_specs=(
            P(("row", "col", "depth"), None),
            P(("col", "depth", "row"), None),
            P(("col", "depth")),
            P("row"),
            P("row"),
        ),
        out_specs=(P(("row", "col", "depth"), None), P(("col", "depth", "row"), None)),
        check_vma=False,
    )
```

profile of v0, /device:TPU:0, one launch (start us, length us, event | category | flops | bytes accessed | tf_op | source)
XLA Modules:
  0.0 161.2 jit_solution(11841545412863525617)
XLA Ops:
  7.2 0.0 all-gather.15.cloned.1.call-start
  7.2 0.7 all-gather.15.cloned.1.call-update
  7.9 0.0 all-gather.17.cloned.1.call-start
  7.9 29.2 %all_gather.45 = bf16[512,256]{1,0:T(8,128)(2,1)} all-gather(bf16[64,256]{1,0:T(8,128)(2,1)} %param.9), channel_id=1, replica_groups=mesh['row'=4,'col'=2,'depth'=4] {'col','depth'}, dimensions={0}, use_global_device_ids=true | all-gather | bytes 294912 | tf_op jit(solution)/shard_map/all_gather | solution.py:45
  37.1 0.0 all-gather.17.cloned.1.call-update
  37.1 0.0 reduce-scatter.2.cloned.1.call-start
  37.2 0.8 fusion.13
  38.0 0.7 convert_element_type.28
  38.7 0.8 fusion.14
  39.4 8.2 %all-gather.8 = f32[4,1,512]{2,1,0:T(1,128)S(1)} all-gather(f32[1,1,512]{2,1,0:T(1,128)} %bitcast.61), channel_id=1, replica_groups=mesh['row'=4,'col'=2,'depth'=4] {'row'}, dimensions={0}, use_global_device_ids=true | all-gather | bytes 10240 | tf_op jit(solution)/shard_map/all_gather | solution.py:90
  47.7 8.1 %all-gather.11 = f32[4,1,512]{2,1,0:T(1,128)S(1)} all-gather(f32[1,1,512]{2,1,0:T(1,128)S(1)} %bitcast.62), channel_id=1, replica_groups=mesh['row'=4,'col'=2,'depth'=4] {'row'}, dimensions={0}, use_global_device_ids=true | all-gather | bytes 10240 | tf_op jit(solution)/shard_map/all_gather | solution.py:91
  55.7 0.8 dynamic_slice.16
  56.5 1.9 %fusion.16 = (f32[256]{0:T(256)S(1)}, f32[256,2048]{1,0:T(8,128)S(1)}) fusion(f32[2048]{0:T(1024)} %param.11, bf16[2048,256]{1,0:T(8,128)(2,1)} %all-gather.15.cloned.1.call-done, bf16[512,256]{1,0:T(8,128)(2,1)} %all_gather.45), kind=kOutput, calls=%fused_computation.39 | convolution fusion | flops 270008064 | bytes 3286016 | tf_op jit(solution)/shard_map/id,jd->ij/dot_general | solution.py:27
  58.4 14.5 %all-gather.6 = f32[8,1,256]{2,1,0:T(1,128)S(1)} all-gather(f32[1,1,256]{2,1,0:T(1,128)S(1)} %bitcast.57), channel_id=4, replica_groups=mesh['row'=4,'col'=2,'depth'=4] {'col','depth'}, dimensions={0}, use_global_device_ids=true | all-gather | bytes 9216 | tf_op jit(solution)/shard_map/all_gather | solution.py:13
  72.9 0.4 exponential_reduce_fusion
  73.4 13.3 %all-gather.7 = f32[8,1,256]{2,1,0:T(1,128)S(1)} all-gather(f32[1,1,256]{2,1,0:T(1,128)S(1)} %bitcast.66), channel_id=5, replica_groups=mesh['row'=4,'col'=2,'depth'=4] {'col','depth'}, dimensions={0}, use_global_device_ids=true | all-gather | bytes 9216 | tf_op jit(solution)/shard_map/all_gather | solution.py:13
  86.7 0.6 fusion.15
  87.3 0.0 slice-start.1
  87.3 14.9 %all-gather.4 = f32[8,1,256]{2,1,0:T(1,128)S(1)} all-gather(f32[1,1,256]{2,1,0:T(1,128)S(1)} %bitcast.58), channel_id=2, replica_groups=mesh['row'=4,'col'=2,'depth'=4] {'col','depth'}, dimensions={0}, use_global_device_ids=true | all-gather | bytes 9216 | tf_op jit(solution)/shard_map/all_gather | solution.py:13
  102.3 0.4 exponential_reduce_fusion.1
  102.7 13.1 %all-gather.5 = f32[8,1,256]{2,1,0:T(1,128)S(1)} all-gather(f32[1,1,256]{2,1,0:T(1,128)S(1)} %bitcast.67), channel_id=3, replica_groups=mesh['row'=4,'col'=2,'depth'=4] {'col','depth'}, dimensions={0}, use_global_device_ids=true | all-gather | bytes 9216 | tf_op jit(solution)/shard_map/all_gather | solution.py:13
  115.8 0.3 while.25
  116.2 0.3 while.24
  116.6 2.8 %multiply_convert_fusion.2 = (bf16[256,2048]{1,0:T(8,128)(2,1)S(1)}, bf16[256,2048]{1,0:T(8,128)(2,1)S(1)}) fusion(f32[256,2048]{1,0:T(8,128)} %copy-done, s32[2048]{0:T(1024)S(1)} %iota_add_fusion, f32[256]{0:T(256)S(1)} %get-tuple-element.101, f32[256]{0:T(256)S(1)} %get-tuple-element.94, s32[256]{0:T(256)S(1)} %get-tuple-element.92, ...), kind=kLoop, calls=%fused_computation.17 | loop fusion | flops 6291456 | bytes 6305792 | tf_op jit(solution)/shard_map/convert_element_type | solution.py:41
  119.3 0.0 copy-start.3
  119.4 1.5 fusion.6
  120.9 0.0 reduce-scatter.2.cloned.1.call-update
  120.9 7.1 %all-gather.9 = f32[4,1,512]{2,1,0:T(1,128)S(1)} all-gather(f32[1,1,512]{2,1,0:T(1,128)S(1)} %bitcast.63), channel_id=1, replica_groups=mesh['row'=4,'col'=2,'depth'=4] {'row'}, dimensions={0}, use_global_device_ids=true | all-gather | bytes 10240 | tf_op jit(solution)/shard_map/all_gather | solution.py:88
  128.1 8.0 %all-gather.10 = f32[4,1,512]{2,1,0:T(1,128)S(1)} all-gather(f32[1,1,512]{2,1,0:T(1,128)S(1)} %bitcast.64), channel_id=1, replica_groups=mesh['row'=4,'col'=2,'depth'=4] {'row'}, dimensions={0}, use_global_device_ids=true | all-gather | bytes 10240 | tf_op jit(solution)/shard_map/all_gather | solution.py:89
  136.1 0.0 all-gather.17.cloned.1.call-done
  136.2 4.7 %convolution_multiply_fusion.2 = f32[512,256]{1,0:T(8,128)} fusion(bf16[2048,256]{1,0:T(8,128)(2,1)} %all-gather.17.cloned.1.call-done, bf16[512,256]{1,0:T(8,128)(2,1)S(1)} %copy-done.3, s32[512]{0:T(512)S(1)} %iota_add_fusion.1, f32[2048]{0:T(1024)S(1)} %bitcast.59, f32[512]{0:T(512)S(1)} %dynamic_slice.16, f32[2048]{0:T(1024)S(1)} %bitcast.60, ...), kind=kOutput, calls=%fused_computation.19 | convolution fusion | flops 1082261504 | bytes 1863680 | tf_op jit(solution)/shard_map/ij,id->jd/dot_general | solution.py:103
  140.9 13.8 %reduce-scatter.2.cloned.1.call-done = f32[64,256]{1,0:T(8,128)} async-done(((f32[512,256]{1,0:T(8,128)}), f32[64,256]{1,0:T(8,128)}) %reduce-scatter.2.cloned.1.call-update) | async-done | bytes 65552 | tf_op jit(solution)/shard_map/reduce_scatter | solution.py:76
  (60 shorter events, 0.5 us)
Async XLA Ops:
  7.2 49.4 %all-gather.15.cloned.1.call-start = ((), (), s32[]{:S(2)}) async-start(), calls=%async_computation.1 | async-start | bytes 1310720 | tf_op jit(solution)/shard_map/all_gather | solution.py:46
  7.9 128.3 %all-gather.17.cloned.1.call-start = ((), (), s32[]{:S(2)}) async-start(), calls=%async_computation.3 | async-start | bytes 1310720 | tf_op jit(solution)/shard_map/all_gather | solution.py:122
  37.1 117.5 %reduce-scatter.2.cloned.1.call-start = ((), (), s32[]{:S(2)}) async-start(), calls=%async_computation.2 | async-start | bytes 589824 | tf_op jit(solution)/shard_map/reduce_scatter | solution.py:76
  56.5 30.2 %copy-start.2 = (bf16[512,256]{1,0:T(8,128)(2,1)S(1)}, bf16[512,256]{1,0:T(8,128)(2,1)}, u32[]{:S(2)}) copy-start(bf16[512,256]{1,0:T(8,128)(2,1)} %all_gather.45) | copy-start | bytes 786436
  56.5 30.2 %copy-start.5 = (f32[2048]{0:T(1024)S(1)}, f32[2048]{0:T(1024)}, u32[]{:S(2)}) copy-start(f32[2048]{0:T(1024)} %param.11) | copy-start | bytes 24580
  56.5 30.2 %copy-start.1 = (bf16[2048,256]{1,0:T(8,128)(2,1)S(1)}, bf16[2048,256]{1,0:T(8,128)(2,1)}, u32[]{:S(2)}) copy-start(bf16[2048,256]{1,0:T(8,128)(2,1)} %all-gather.15.cloned.1.call-done) | copy-start | bytes 3145732
  72.9 14.3 %copy-start.4 = (f32[8,1,256]{2,1,0:T(1,128)}, f32[8,1,256]{2,1,0:T(1,128)S(1)}, u32[]{:S(2)}) copy-start(f32[8,1,256]{2,1,0:T(1,128)S(1)} %all-gather.6) | copy-start | bytes 24580
  87.3 15.0 %copy-start = (f32[256,2048]{1,0:T(8,128)}, f32[256,2048]{1,0:T(8,128)S(1)}, u32[]{:S(2)}) copy-start(f32[256,2048]{1,0:T(8,128)S(1)} %get-tuple-element.97) | copy-start | bytes 6291460
  87.3 28.5 %slice-start.1 = ((f32[8,1,256]{2,1,0:T(1,128)}), f32[7,1,256]{2,1,0:T(1,128)S(1)}, s32[]{:S(2)}) async-start(f32[8,1,256]{2,1,0:T(1,128)} %copy-done.4), calls=%async_computation.5 | async-start | bytes 14336 | tf_op jit(solution)/shard_map/slice | solution.py:15
  87.3 28.5 %slice-start = ((f32[8,1,256]{2,1,0:T(1,128)}), f32[1,1,256]{2,1,0:T(1,128)S(1)}, s32[]{:S(2)}) async-start(f32[8,1,256]{2,1,0:T(1,128)} %copy-done.4), calls=%async_computation.4 | async-start | bytes 2048 | tf_op jit(solution)/shard_map/slice | solution.py:14
  119.3 16.8 %copy-start.3 = (bf16[512,256]{1,0:T(8,128)(2,1)S(1)}, bf16[512,256]{1,0:T(8,128)(2,1)}, u32[]{:S(2)}) copy-start(bf16[512,256]{1,0:T(8,128)(2,1)} %param.10) | copy-start | bytes 786436
Sparse Core Ops, SparseCore 0:
  9.8 29.2 all-gather.14
  40.9 26.5 all-gather.16
  121.0 33.5 reduce-scatter.1
where the time goes:
time: 162 us; the launch traced here: 161 us
  blocking collectives  117 us (72%)
  waiting for transfers between devices  14.5 us (9%)
  between operations  13.9 us (9%)
  matrix products  8.64 us (5%)
  other arithmetic  4.65 us (3%)
  local copies, waits for them, and re-layouts  2.46 us (2%)
    all_gather x4, blocking collectives, combined_all(): pieces = jax.tree.map(lambda part: lax.all_gather(part, axis), value)  55.9 us
    all_gather x1, blocking collectives, per_device(): sources = lax.all_gather(source_desc, ('col', 'depth'), axis=0, tiled=True)  29.2 us
    reduce_scatter x1, waiting for transfers between devices, per_device(): lax.psum_scatter(score_scale * jnp.dot(delta_all, targets, preferred_elem...  13.8 us
    all_gather x1, blocking collectives, per_device(): lax.all_gather(row_weight, 'row', axis=0, tiled=True)  8.23 us
    all_gather x1, blocking collectives, per_device(): lax.all_gather(match_float, 'row', axis=0, tiled=True)  8.07 us
    all_gather x1, blocking collectives, per_device(): lax.all_gather(all_mass, 'row', axis=0, tiled=True)  8.05 us
    all_gather x1, blocking collectives, per_device(): lax.all_gather(all_highest, 'row', axis=0, tiled=True)  7.14 us
    dot_general x1, matrix products, block_term(): jnp.einsum('ij,id->jd', delta_block, rows_block, preferred_element_type=j...  4.69 us
  transfers between devices with their start and end apart: 3, of which 1 were waited for; matrix products, arithmetic and copies ran while one was open for 10% of the time, Pallas kernels for 0%

commit v1 on v0

v1 whole, which is shorter than its diff:
```python
import functools
import jax
import jax.numpy as jnp
from jax import lax
from jax.experimental import pallas as pl
from jax.experimental.pallas import tpu as pltpu
from jax.sharding import PartitionSpec as P

score_scale = 0.1875
F32 = jnp.float32
BF16 = jnp.bfloat16


def kernel(R, NC, ND, src, tgt, dual, wm, gs_out, gt_out,
           S, T2, dual2, wm_all, dcol, e_buf, m_buf, lamz, lamx, lamz_c, dbuf, ps, px, zs, zr,
           own_part, gt_send, gt_recv,
           s_pair, r_pair, s_z, r_z, s_x, r_x, s_wm, r_wm, s_lz, r_lz, s_lx, r_lx, s_p, r_p, s_zp, r_zp):
    G = (NC // 2) * ND
    n, D = src.shape
    own = tgt.shape[0]
    C = G * n
    row = lax.axis_index("row")
    col = lax.axis_index("col")
    dep = lax.axis_index("depth")
    par = lax.rem(col, 2)
    grp = (col // 2) * ND + dep
    sib_col = col + 1 - 2 * par

    def dev(r, c, d):
        return {"row": r, "col": c, "depth": d}

    sib = dev(row, sib_col, dep)

    def xpeer(k):
        r = lax.rem(row + k, R)
        return r, dev(r, col, dep)

    def zpeer(k):
        g = lax.rem(grp + k, G)
        return g, dev(row, (g // ND) * 2 + par, lax.rem(g, ND))

    def rcopy(a, b, ss, rs, to):
        return pltpu.make_async_remote_copy(src_ref=a, dst_ref=b, send_sem=ss, recv_sem=rs,
                                            device_id=to, device_id_type=pl.DeviceIdType.MESH)

    barrier = pltpu.get_barrier_semaphore()
    peers = [sib] + [xpeer(k)[1] for k in range(1, R)] + [zpeer(k)[1] for k in range(1, G)]
    for p in peers:
        pl.semaphore_signal(barrier, inc=1, device_id=p, device_id_type=pl.DeviceIdType.MESH)

    S[row, grp] = src[...]
    wm_all[row] = wm[...]
    dcol[0:own, :] = jnp.transpose(jnp.broadcast_to(dual[...], (128, own)))
    pl.semaphore_wait(barrier, len(peers))

    sends = []

    def go(c):
        c.start()
        sends.append(c)

    for k in range(1, G):
        g, to = zpeer(k)
        go(rcopy(src, S.at[row, grp], s_z.at[k], r_z.at[grp], to))
    for k in range(1, R):
        r, to = xpeer(k)
        go(rcopy(src, S.at[row, grp], s_x.at[k, 0], r_x.at[row, grp], to))
    go(rcopy(tgt, T2, s_pair.at[0], r_pair.at[0], sib))
    go(rcopy(dual, dual2, s_pair.at[1], r_pair.at[1], sib))
    for k in range(1, R):
        r, to = xpeer(k)
        go(rcopy(wm, wm_all.at[row], s_wm.at[k], r_wm.at[row], to))

    for k in range(1, G):
        g, to = zpeer(k)
        rcopy(src, S.at[row, g], s_z.at[k], r_z.at[g], to).wait_recv()
        for j in range(1, R):
            r, xto = xpeer(j)
            go(rcopy(S.at[row, g], S.at[row, g], s_x.at[j, k], r_x.at[row, g], xto))

    rcopy(dual, dual2, s_pair.at[1], r_pair.at[1], sib).wait_recv()
    dcol[own:2 * own, :] = jnp.transpose(jnp.broadcast_to(dual2[...], (128, own)))
    rcopy(tgt, T2, s_pair.at[0], r_pair.at[0], sib).wait_recv()

    lane_rep = C // 128

    def scores_chunk(r):
        rows = S[r].reshape(C, D)
        tops = []
        for h, t in ((0, tgt), (1, T2)):
            p = lax.dot_general(t[...], rows, (((1,), (1,)), ((), ())), preferred_element_type=F32)
            dc = dcol[h * own:(h + 1) * own, :]
            s = score_scale * p + jnp.concatenate([dc] * lane_rep, axis=1)
            e_buf[r, h * own:(h + 1) * own, :] = s
            tops.append(jnp.max(s, axis=0, keepdims=True))
        top = jnp.maximum(tops[0], tops[1])
        m_buf[r] = top
        e = jnp.exp(e_buf[r] - top)
        e_buf[r] = e
        lamz[grp, r] = top + jnp.log(jnp.sum(e, axis=0, keepdims=True))

    scores_chunk(row)

    def chunk_step(k, carry):
        r, to = xpeer(k)
        for g in range(G):
            rcopy(src, S.at[r, g], s_x.at[0, 0], r_x.at[r, g], to).wait_recv()
        scores_chunk(r)
        return carry

    lax.fori_loop(1, R, chunk_step, 0)

    def lse(parts):
        top = functools.reduce(jnp.maximum, parts)
        return top + jnp.log(functools.reduce(jnp.add, [jnp.exp(p - top) for p in parts]))

    for k in range(1, G):
        g, to = zpeer(k)
        go(rcopy(lamz.at[grp], lamz.at[grp], s_lz.at[k], r_lz.at[grp], to))
    for k in range(1, G):
        g, to = zpeer(k)
        rcopy(lamz.at[g], lamz.at[g], s_lz.at[k], r_lz.at[g], to).wait_recv()
    lamx[row] = lse([lamz[g] for g in range(G)])
    for k in range(1, R):
        r, to = xpeer(k)
        go(rcopy(lamx.at[row], lamx.at[row], s_lx.at[k], r_lx.at[row], to))
    for k in range(1, R):
        r, to = xpeer(k)
        rcopy(wm, wm_all.at[r], s_wm.at[k], r_wm.at[r], to).wait_recv()
        rcopy(lamx.at[r], lamx.at[r], s_lx.at[k], r_lx.at[r], to).wait_recv()
    lamz_c[...] = lse([lamx[r] for r in range(R)])

    first = [((c * ND + dep) * R + row) * own for c in (col, sib_col)]

    def delta_chunk(r):
        w = wm_all[r, 0:1, :]
        match = wm_all[r, 1:2, :].astype(jnp.int32)
        scale = w * jnp.exp(m_buf[r] - lamz_c[r])
        part = None
        for h, t in ((0, tgt), (1, T2)):
            ids = lax.broadcasted_iota(jnp.int32, (own, C), 0)
            hit = jnp.where(ids == match - first[h], w, 0.0)
            d = (scale * e_buf[r, h * own:(h + 1) * own, :] - hit).astype(BF16)
            dbuf[r, h * own:(h + 1) * own, :] = d
            q = lax.dot_general(d, t[...], (((0,), (0,)), ((), ())), preferred_element_type=F32)
            part = q if part is None else part + q
        return part

    def part_step(k, carry):
        r, to = xpeer(k)
        ps[r] = delta_chunk(r).astype(BF16).reshape(G, n, D)
        for g in range(G):
            rcopy(ps.at[r, g], px.at[row, g], s_p.at[k, g], r_p.at[row, g], to).start()
        return carry

    lax.fori_loop(1, R, part_step, 0)
    own_part[...] = delta_chunk(row).reshape(G, n, D)

    def gt_half(h):
        def add(r, acc):
            return acc + jnp.dot(dbuf[r, h * own:(h + 1) * own, :], S[r].reshape(C, D),
                                 preferred_element_type=F32)
        acc = jnp.dot(dbuf[0, h * own:(h + 1) * own, :], S[0].reshape(C, D), preferred_element_type=F32)
        for r in range(1, R):
            acc = add(r, acc)
        return acc

    gt_send[...] = gt_half(1)
    go(rcopy(gt_send, gt_recv, s_pair.at[2], r_pair.at[2], sib))

    def stage_sum(g):
        acc = own_part[g]
        for k in range(1, R):
            r, to = xpeer(k)
            rcopy(ps.at[r, g], px.at[r, g], s_p.at[k, g], r_p.at[r, g], to).wait_recv()
            acc = acc + px[r, g].astype(F32)
        return acc

    for k in range(1, G):
        g, to = zpeer(k)
        zs[g] = stage_sum(g).astype(BF16)
        go(rcopy(zs.at[g], zr.at[grp], s_zp.at[k], r_zp.at[grp], to))
    mine = stage_sum(grp)

    gt_out[...] = gt_half(0)
    rcopy(gt_send, gt_recv, s_pair.at[2], r_pair.at[2], sib).wait_recv()
    gt_out[...] = score_scale * (gt_out[...] + gt_recv[...])

    for k in range(1, G):
        g, to = zpeer(k)
        rcopy(zs.at[g], zr.at[g], s_zp.at[k], r_zp.at[g], to).wait_recv()
        mine = mine + zr[g].astype(F32)
    gs_out[...] = score_scale * mine

    for c in sends:
        c.wait_send()
    for k in range(1, R):
        r, to = xpeer(k)
        for g in range(G):
            rcopy(ps.at[r, g], px.at[row, g], s_p.at[k, g], r_p.at[row, g], to).wait_send()


def per_device(R, NC, ND, source_desc, target_desc, target_dual, row_weight, matches):
    n, D = source_desc.shape
    own = target_desc.shape[0]
    G = (NC // 2) * ND
    C = G * n
    par = lax.rem(lax.axis_index("col"), 2)
    dual = lax.dynamic_slice_in_dim(target_dual, lax.axis_index("row") * own, own, 0)[None, :]
    wm = jnp.stack([row_weight, matches.astype(F32)]).reshape(2, NC // 2, 2, ND * n)
    wm = lax.dynamic_index_in_dim(wm, par, 2, keepdims=False).reshape(2, C)
    vm = pl.BlockSpec(memory_space=pltpu.VMEM)
    dma = pltpu.SemaphoreType.DMA
    return pl.pallas_call(
        functools.partial(kernel, R, NC, ND),
        out_shape=(jax.ShapeDtypeStruct((n, D), F32), jax.ShapeDtypeStruct((own, D), F32)),
        in_specs=[vm] * 4,
        out_specs=(vm, vm),
        scratch_shapes=[
            pltpu.VMEM((R, G, n, D), BF16),
            pltpu.VMEM((own, D), BF16),
            pltpu.VMEM((1, own), F32),
            pltpu.VMEM((R, 2, C), F32),
            pltpu.VMEM((2 * own, 128), F32),
            pltpu.VMEM((R, 2 * own, C), F32),
            pltpu.VMEM((R, 1, C), F32),
            pltpu.VMEM((G, R, 1, C), F32),
            pltpu.VMEM((R, R, 1, C), F32),
            pltpu.VMEM((R, 1, C), F32),
            pltpu.VMEM((R, 2 * own, C), BF16),
            pltpu.VMEM((R, G, n, D), BF16),
            pltpu.VMEM((R, G, n, D), BF16),
            pltpu.VMEM((G, n, D), BF16),
            pltpu.VMEM((G, n, D), BF16),
            pltpu.VMEM((G, n, D), F32),
            pltpu.VMEM((own, D), F32),
            pltpu.VMEM((own, D), F32),
            dma((3,)), dma((3,)),
            dma((G,)), dma((G,)),
            dma((R, G)), dma((R, G)),
            dma((R,)), dma((R,)),
            dma((G,)), dma((G,)),
            dma((R,)), dma((R,)),
            dma((R, G)), dma((R, G)),
            dma((G,)), dma((G,)),
        ],
        compiler_params=pltpu.CompilerParams(collective_id=0, has_side_effects=True),
    )(source_desc, target_desc, dual, wm)


def solution(mesh):
    R, NC, ND = mesh.shape["row"], mesh.shape["col"], mesh.shape["depth"]
    return jax.shard_map(
        functools.partial(per_device, R, NC, ND),
        mesh=mesh,
        in_specs=(
            P(("row", "col", "depth"), None),
            P(("col", "depth", "row"), None),
            P(("col", "depth")),
            P("row"),
            P("row"),
        ),
        out_specs=(P(("row", "col", "depth"), None), P(("col", "depth", "row"), None)),
        check_vma=False,
    )
```

time: 162 us -> 42.3 us (0.26)
  blocking collectives: 117 us -> 0 us
  Pallas kernels: 0 us -> 35.4 us
  waiting for transfers between devices: 14.5 us -> 0 us
  between operations: 13.9 us -> 0.66 us
  matrix products: 8.64 us -> 0 us
  other arithmetic: 4.65 us -> 0.59 us
  local copies, waits for them, and re-layouts: 2.46 us -> 5.37 us
    all_gather x9 -> x0, blocking collectives: 117 us -> none  [the longest x4 55.9 us: combined_all(): pieces = jax.tree.map(lambda part: lax.all_gather(part, axis), value)]
    pallas_call x0 -> x1, Pallas kernels: none -> 35.4 us  [per_device(): pl.pallas_call(functools.partial(kernel, R, NC, ND), out_shape=(jax.Shape...]
    reduce_scatter x1 -> x0, waiting for transfers between devices: 13.8 us -> none  [per_device(): lax.psum_scatter(score_scale * jnp.dot(delta_all, targets, preferred_elem...]
    dot_general x4 -> x0, matrix products: 8.64 us -> none  [the longest x1 4.69 us: block_term(): jnp.einsum('ij,id->jd', delta_block, rows_block, preferred_element_type=j...]
    unnamed x16 -> x6, local copies, waits for them, and re-layouts: 0.03 us -> 4.02 us
    convert_element_type x3 -> x1, other arithmetic: 3.45 us -> 0.01 us  [per_device(): matches.astype(F32)]
  transfers between devices with their start and end apart: 3 -> 0, of which waited for: 1 -> 0; matrix products, arithmetic and copies ran while one was open for 10% -> 0% of each run, Pallas kernels for 0% -> 0%
where the time goes in v1:
time: 42.3 us; the launch traced here: 42.1 us
  Pallas kernels  35.4 us (84%)
  local copies, waits for them, and re-layouts  5.37 us (13%)
  between operations  0.66 us (2%)
  other arithmetic  0.59 us (1%)
    pallas_call x1, Pallas kernels, per_device(): pl.pallas_call(functools.partial(kernel, R, NC, ND), out_shape=(jax.Shape...  35.4 us
    unnamed x6, local copies, waits for them, and re-layouts  4.02 us
    dynamic_slice x1, local copies, waits for them, and re-layouts, per_device(): lax.dynamic_slice_in_dim(target_dual, lax.axis_index('row') * own, own, 0)  1.34 us

profile of v1, /device:TPU:0, one launch (start us, length us, event | category | flops | bytes accessed | tf_op | source)
XLA Modules:
  0.0 42.1 jit_solution(6190120892743863832)
XLA Ops:
  0.6 0.0 copy-start
  0.7 1.3 %dynamic_slice.7 = f32[512]{0:T(512)} dynamic-slice(f32[2048]{0:T(1024)} %param.7, s32[]{:T(128)S(6)} %select_n.7), dynamic_slice_sizes={512} | dynamic-slice | bytes 4100 | tf_op jit(solution)/shard_map/dynamic_slice | solution.py:209
  2.0 0.0 copy-done
  2.0 0.0 copy-start.1
  2.0 0.7 %copy-done.1 = f32[512]{0:T(512)S(1)} copy-done((f32[512]{0:T(512)S(1)}, f32[512]{0:T(512)}, u32[]{:S(2)}) %copy-start.1) | copy-done | bytes 2072
  2.7 0.6 %fusion.1.wm = f32[2,256]{1,0:T(2,128)} fusion(s32[]{:T(128)S(6)} %select_n.8, f32[1,1,2,256]{3,0,2,1:T(1,128)S(1)} %bitcast.7, f32[1,1,2,256]{3,0,2,1:T(1,128)S(1)} %bitcast.6), kind=kLoop, calls=%fused_computation.3 | loop fusion | flops 512 | bytes 6148 | tf_op jit(solution)/shard_map/reshape | solution.py:211
  3.3 35.4 %shard_map.68 = (f32[64,256]{1,0:T(8,128)}, f32[512,256]{1,0:T(8,128)}) custom-call(bf16[64,256]{1,0:T(8,128)(2,1)} %src.1, bf16[512,256]{1,0:T(8,128)(2,1)} %tgt.1, f32[1,512]{1,0:T(1,128)} %bitcast.5, f32[2,256]{1,0:T(2,128)} %fusion.1.wm), custom_call_target="tpu_custom_call" | custom-call | tf_op jit(solution)/shard_map/pallas_call | solution.py:214
  38.7 1.5 %copy.9 = f32[64,256]{1,0:T(8,128)} copy(f32[64,256]{1,0:T(8,128)} %get-tuple-element.4) | data formatting | bytes 131072
  40.2 1.9 %copy.10 = f32[512,256]{1,0:T(8,128)} copy(f32[512,256]{1,0:T(8,128)} %get-tuple-element.5) | data formatting | bytes 1048576
  (1 shorter events, 0.0 us)
Async XLA Ops:
  0.6 1.4 %copy-start = (s32[512]{0:T(512)S(1)}, s32[512]{0:T(512)}, u32[]{:S(2)}) copy-start(s32[512]{0:T(512)} %param.9) | copy-start | bytes 6148
  2.0 0.7 %copy-start.1 = (f32[512]{0:T(512)S(1)}, f32[512]{0:T(512)}, u32[]{:S(2)}) copy-start(f32[512]{0:T(512)} %param.8) | copy-start | bytes 6148

commit v2 on v1

v2 whole, which is shorter than its diff:
```python
import functools
import jax
import jax.numpy as jnp
from jax import lax
from jax.experimental import pallas as pl
from jax.experimental.pallas import tpu as pltpu
from jax.sharding import PartitionSpec as P

score_scale = 0.1875
F32 = jnp.float32
BF16 = jnp.bfloat16


def kernel(R, NC, ND, src, tgt, dual_all, weight, match_in, gs_out, gt_out,
           S, T2, dual, dual2, wm, wm_all, wm_g, dcol, e_buf, m_buf, lamz, lamx, lamz_c, dbuf, ps, px, zs, zr,
           partf, gt_send, gt_recv,
           s_pair, r_pair, s_z, r_z, s_x, r_x, s_wm, r_wm, s_lz, r_lz, s_lx, r_lx, s_p, r_p, s_zp, r_zp):
    G = (NC // 2) * ND
    n, D = src.shape
    own = tgt.shape[0]
    C = R * n
    row = lax.axis_index("row")
    col = lax.axis_index("col")
    dep = lax.axis_index("depth")
    par = lax.rem(col, 2)
    grp = (col // 2) * ND + dep
    sib_col = col + 1 - 2 * par

    def dev(r, c, d):
        return {"row": r, "col": c, "depth": d}

    sib = dev(row, sib_col, dep)

    def xpeer(k):
        r = lax.rem(row + k, R)
        return r, dev(r, col, dep)

    def zpeer(k):
        g = grp
        if G & (G - 1):
            g = lax.rem(grp + k, G)
        else:
            bit = 1
            while bit < G:
                if k & bit:
                    g = g + bit - 2 * bit * lax.rem(g // bit, 2)
                bit *= 2
        return g, dev(row, (g // ND) * 2 + par, lax.rem(g, ND))

    def rcopy(a, b, ss, rs, to):
        return pltpu.make_async_remote_copy(src_ref=a, dst_ref=b, send_sem=ss, recv_sem=rs,
                                            device_id=to, device_id_type=pl.DeviceIdType.MESH)

    barrier = pltpu.get_barrier_semaphore()
    peers = [sib] + [xpeer(k)[1] for k in range(1, R)] + [zpeer(k)[1] for k in range(1, G)]
    for p in peers:
        pl.semaphore_signal(barrier, inc=1, device_id=p, device_id_type=pl.DeviceIdType.MESH)

    S[grp, row] = src[...]
    dual[...] = dual_all[:, pl.ds(pl.multiple_of(row * own, own), own)]
    dcol[0:own, :] = jnp.transpose(jnp.broadcast_to(dual[...], (128, own)))
    for i, vec in ((0, weight[...]), (1, match_in[...].astype(F32))):
        span = ND * n
        parts = [jnp.where(par == 0, vec[:, 2 * c * span:(2 * c + 1) * span],
                           vec[:, (2 * c + 1) * span:(2 * c + 2) * span]) for c in range(NC // 2)]
        wm[i:i + 1, :] = parts[0] if len(parts) == 1 else jnp.concatenate(parts, axis=1)
    wm_all[row] = wm[...]
    pl.semaphore_wait(barrier, len(peers))

    sends = []

    def go(c):
        c.start()
        sends.append(c)

    for k in range(1, G):
        g, to = zpeer(k)
        go(rcopy(src, S.at[grp, row], s_z.at[k], r_z.at[grp], to))
    for k in range(1, R):
        r, to = xpeer(k)
        go(rcopy(src, S.at[grp, row], s_x.at[k, 0], r_x.at[row, grp], to))
    go(rcopy(tgt, T2, s_pair.at[0], r_pair.at[0], sib))
    go(rcopy(dual, dual2, s_pair.at[1], r_pair.at[1], sib))

    def forward(k):
        g, to = zpeer(k)
        rcopy(src, S.at[g, row], s_z.at[k], r_z.at[g], to).wait_recv()
        for j in range(1, R):
            r, xto = xpeer(j)
            go(rcopy(S.at[g, row], S.at[g, row], s_x.at[j, k], r_x.at[row, g], xto))

    forward(1)
    for k in range(1, R):
        r, to = xpeer(k)
        go(rcopy(wm, wm_all.at[row], s_wm.at[k], r_wm.at[row], to))
    rcopy(dual, dual2, s_pair.at[1], r_pair.at[1], sib).wait_recv()
    dcol[own:2 * own, :] = jnp.transpose(jnp.broadcast_to(dual2[...], (128, own)))
    rcopy(tgt, T2, s_pair.at[0], r_pair.at[0], sib).wait_recv()

    lane_rep = C // 128

    def scores_chunk(g):
        rows = S[g].reshape(C, D)
        tops = []
        for h, t in ((0, tgt), (1, T2)):
            p = lax.dot_general(t[...], rows, (((1,), (1,)), ((), ())), preferred_element_type=F32)
            dc = dcol[h * own:(h + 1) * own, :]
            s = score_scale * p + jnp.concatenate([dc] * lane_rep, axis=1)
            e_buf[g, h * own:(h + 1) * own, :] = s
            tops.append(jnp.max(s, axis=0, keepdims=True))
        top = jnp.maximum(tops[0], tops[1])
        m_buf[g] = top
        e = jnp.exp(e_buf[g] - top)
        e_buf[g] = e
        lamz[grp, g] = top + jnp.log(jnp.sum(e, axis=0, keepdims=True))

    for k in range(G):
        g = zpeer(k)[0]
        if 2 <= k + 1 < G:
            forward(k + 1)
        for j in range(1, R):
            r, to = xpeer(j)
            rcopy(src, S.at[g, r], s_x.at[0, 0], r_x.at[r, g], to).wait_recv()
        scores_chunk(g)

    def lse(parts):
        top = functools.reduce(jnp.maximum, parts)
        return top + jnp.log(functools.reduce(jnp.add, [jnp.exp(p - top) for p in parts]))

    for k in range(1, G):
        g, to = zpeer(k)
        go(rcopy(lamz.at[grp], lamz.at[grp], s_lz.at[k], r_lz.at[grp], to))
    for k in range(1, G):
        g, to = zpeer(k)
        rcopy(lamz.at[g], lamz.at[g], s_lz.at[k], r_lz.at[g], to).wait_recv()
    lamx[row] = lse([lamz[g] for g in range(G)])
    for k in range(1, R):
        r, to = xpeer(k)
        go(rcopy(lamx.at[row], lamx.at[row], s_lx.at[k], r_lx.at[row], to))
    for k in range(1, R):
        r, to = xpeer(k)
        rcopy(wm, wm_all.at[r], s_wm.at[k], r_wm.at[r], to).wait_recv()
    for g in range(G):
        for i in range(2):
            wm_g[g, i:i + 1, :] = jnp.concatenate(
                [wm_all[r, i:i + 1, g * n:(g + 1) * n] for r in range(R)], axis=1)
    for k in range(1, R):
        r, to = xpeer(k)
        rcopy(lamx.at[r], lamx.at[r], s_lx.at[k], r_lx.at[r], to).wait_recv()
    lamz_c[...] = lse([lamx[r] for r in range(R)])

    first = [((c * ND + dep) * R + row) * own for c in (col, sib_col)]

    def delta_chunk(g):
        w = wm_g[g, 0:1, :]
        match = wm_g[g, 1:2, :].astype(jnp.int32)
        scale = w * jnp.exp(m_buf[g] - lamz_c[g])
        part = None
        for h, t in ((0, tgt), (1, T2)):
            ids = lax.broadcasted_iota(jnp.int32, (own, C), 0)
            hit = jnp.where(ids == match - first[h], w, 0.0)
            d = (scale * e_buf[g, h * own:(h + 1) * own, :] - hit).astype(BF16)
            dbuf[g, h * own:(h + 1) * own, :] = d
            q = lax.dot_general(d, t[...], (((0,), (0,)), ((), ())), preferred_element_type=F32)
            part = q if part is None else part + q
        return part

    for kz in range(G - 1, -1, -1):
        g = zpeer(kz)[0]
        part = delta_chunk(g).reshape(R, n, D)
        partf[g] = part
        ps[g] = part.astype(BF16)
        for k in range(1, R):
            r, to = xpeer(k)
            go(rcopy(ps.at[g, r], px.at[g, row], s_p.at[k, kz], r_p.at[row, g], to))

    def gt_half(h):
        acc = None
        for g in range(G):
            q = jnp.dot(dbuf[g, h * own:(h + 1) * own, :], S[g].reshape(C, D), preferred_element_type=F32)
            acc = q if acc is None else acc + q
        return acc

    gt_send[...] = gt_half(1)
    go(rcopy(gt_send, gt_recv, s_pair.at[2], r_pair.at[2], sib))

    def stage_sum(g):
        acc = partf[g, row]
        for k in range(1, R):
            r, to = xpeer(k)
            rcopy(ps.at[g, r], px.at[g, r], s_p.at[k, 0], r_p.at[r, g], to).wait_recv()
            acc = acc + px[g, r].astype(F32)
        return acc

    for k in range(G - 1, 0, -1):
        g, to = zpeer(k)
        zs[g] = stage_sum(g).astype(BF16)
        go(rcopy(zs.at[g], zr.at[grp], s_zp.at[k], r_zp.at[grp], to))
    mine = stage_sum(grp)

    gt_out[...] = gt_half(0)
    rcopy(gt_send, gt_recv, s_pair.at[2], r_pair.at[2], sib).wait_recv()
    gt_out[...] = score_scale * (gt_out[...] + gt_recv[...])

    for k in range(1, G):
        g, to = zpeer(k)
        rcopy(zs.at[g], zr.at[g], s_zp.at[k], r_zp.at[g], to).wait_recv()
        mine = mine + zr[g].astype(F32)
    gs_out[...] = score_scale * mine

    for c in sends:
        c.wait_send()


def per_device(R, NC, ND, source_desc, target_desc, target_dual, row_weight, matches):
    n, D = source_desc.shape
    own = target_desc.shape[0]
    G = (NC // 2) * ND
    C = R * n
    vm = pl.BlockSpec(memory_space=pltpu.VMEM)
    dma = pltpu.SemaphoreType.DMA
    return pl.pallas_call(
        functools.partial(kernel, R, NC, ND),
        out_shape=(jax.ShapeDtypeStruct((n, D), F32), jax.ShapeDtypeStruct((own, D), F32)),
        in_specs=[vm] * 5,
        out_specs=(vm, vm),
        scratch_shapes=[
            pltpu.VMEM((G, R, n, D), BF16),
            pltpu.VMEM((own, D), BF16),
            pltpu.VMEM((1, own), F32),
            pltpu.VMEM((1, own), F32),
            pltpu.VMEM((2, G * n), F32),
            pltpu.VMEM((R, 2, G * n), F32),
            pltpu.VMEM((G, 2, C), F32),
            pltpu.VMEM((2 * own, 128), F32),
            pltpu.VMEM((G, 2 * own, C), F32),
            pltpu.VMEM((G, 1, C), F32),
            pltpu.VMEM((G, G, 1, C), F32),
            pltpu.VMEM((R, G, 1, C), F32),
            pltpu.VMEM((G, 1, C), F32),
            pltpu.VMEM((G, 2 * own, C), BF16),
            pltpu.VMEM((G, R, n, D), BF16),
            pltpu.VMEM((G, R, n, D), BF16),
            pltpu.VMEM((G, n, D), BF16),
            pltpu.VMEM((G, n, D), BF16),
            pltpu.VMEM((G, R, n, D), F32),
            pltpu.VMEM((own, D), F32),
            pltpu.VMEM((own, D), F32),
            dma((3,)), dma((3,)),
            dma((G,)), dma((G,)),
            dma((R, G)), dma((R, G)),
            dma((R,)), dma((R,)),
            dma((G,)), dma((G,)),
            dma((R,)), dma((R,)),
            dma((R, G)), dma((R, G)),
            dma((G,)), dma((G,)),
        ],
        compiler_params=pltpu.CompilerParams(collective_id=0, has_side_effects=True,
                                             vmem_limit_bytes=32 * 1024 * 1024),
    )(source_desc, target_desc, target_dual[None, :], row_weight[None, :], matches[None, :])


def solution(mesh):
    R, NC, ND = mesh.shape["row"], mesh.shape["col"], mesh.shape["depth"]
    return jax.shard_map(
        functools.partial(per_device, R, NC, ND),
        mesh=mesh,
        in_specs=(
            P(("row", "col", "depth"), None),
            P(("col", "depth", "row"), None),
            P(("col", "depth")),
            P("row"),
            P("row"),
        ),
        out_specs=(P(("row", "col", "depth"), None), P(("col", "depth", "row"), None)),
        check_vma=False,
    )
```

time: 42.3 us -> 38.7 us (0.915)
  Pallas kernels: 35.4 us -> 33.3 us
  local copies, waits for them, and re-layouts: 5.37 us -> 4.51 us
  other arithmetic: 0.59 us -> 0 us
    pallas_call x1, Pallas kernels: 35.4 us -> 33.3 us  [per_device(): pl.pallas_call(functools.partial(kernel, R, NC, ND), out_shape=(jax.Shape...]
    dynamic_slice x1 -> x0, local copies, waits for them, and re-layouts: 1.34 us -> none  [per_device(): lax.dynamic_slice_in_dim(target_dual, lax.axis_index('row') * own, own, 0)]
    reshape x1 -> x0, other arithmetic: 0.58 us -> none  [per_device(): wm = lax.dynamic_index_in_dim(wm, par, 2, keepdims=False).reshape(2, C)]
    unnamed x6 -> x12, local copies, waits for them, and re-layouts: 4.02 us -> 4.51 us
where the time goes in v2:
time: 38.7 us; the launch traced here: 38.4 us
  Pallas kernels  33.3 us (86%)
  local copies, waits for them, and re-layouts  4.51 us (12%)
  between operations  0.66 us (2%)
    pallas_call x1, Pallas kernels, per_device(): pl.pallas_call(functools.partial(kernel, R, NC, ND), out_shape=(jax.Shape...  33.3 us
    unnamed x12, local copies, waits for them, and re-layouts  4.51 us

profile of v2, /device:TPU:0, one launch (start us, length us, event | category | flops | bytes accessed | tf_op | source)
XLA Modules:
  0.0 38.4 jit_solution(1935922497773939754)
XLA Ops:
  0.6 0.0 copy-start.4
  0.6 0.0 copy-start.3
  0.7 0.7 %copy-done.4 = s32[512]{0:T(512)S(1)} copy-done((s32[512]{0:T(512)S(1)}, s32[512]{0:T(512)}, u32[]{:S(2)}) %copy-start.4) | copy-done | bytes 2072
  1.3 0.0 copy-done.3
  1.3 0.0 copy-start
  1.3 0.9 %copy-done = bf16[512,256]{1,0:T(8,128)(2,1)S(1)} copy-done((bf16[512,256]{1,0:T(8,128)(2,1)S(1)}, bf16[512,256]{1,0:T(8,128)(2,1)}, u32[]{:S(2)}) %copy-start) | copy-done | bytes 262168
  2.3 0.0 copy-start.1
  2.3 0.8 %copy-done.1 = bf16[64,256]{1,0:T(8,128)(2,1)S(1)} copy-done((bf16[64,256]{1,0:T(8,128)(2,1)S(1)}, bf16[64,256]{1,0:T(8,128)(2,1)}, u32[]{:S(2)}) %copy-start.1) | copy-done | bytes 32792
  3.0 0.0 copy-start.2
  3.0 0.7 %copy-done.2 = f32[2048]{0:T(1024)S(1)} copy-done((f32[2048]{0:T(1024)S(1)}, f32[2048]{0:T(1024)}, u32[]{:S(2)}) %copy-start.2) | copy-done | bytes 8216
  3.7 33.3 %shard_map.68 = (f32[64,256]{1,0:T(8,128)S(1)}, f32[512,256]{1,0:T(8,128)S(1)}) custom-call(bf16[64,256]{1,0:T(8,128)(2,1)S(1)} %copy-done.1, bf16[512,256]{1,0:T(8,128)(2,1)S(1)} %copy-done, f32[1,2048]{1,0:T(1,128)S(1)} %bitcast.3, f32[1,512]{1,0:T(1,128)S(1)} %bitcast.4, s32[1,512]{1,0:T(1,128)S(1)} %bitcast.5), custom_call_target="tpu_custom_call" | custom-call | tf_op jit(solution)/shard_map/pallas_call | solution.py:222
  37.0 0.6 %copy.9 = f32[64,256]{1,0:T(8,128)} copy(f32[64,256]{1,0:T(8,128)S(1)} %get-tuple-element.4) | data formatting | bytes 131072
  37.6 0.8 %copy.10 = f32[512,256]{1,0:T(8,128)} copy(f32[512,256]{1,0:T(8,128)S(1)} %get-tuple-element.5) | data formatting | bytes 1048576
Async XLA Ops:
  0.6 0.7 %copy-start.4 = (s32[512]{0:T(512)S(1)}, s32[512]{0:T(512)}, u32[]{:S(2)}) copy-start(s32[512]{0:T(512)} %param.9) | copy-start | bytes 6148
  0.6 0.7 %copy-start.3 = (f32[512]{0:T(512)S(1)}, f32[512]{0:T(512)}, u32[]{:S(2)}) copy-start(f32[512]{0:T(512)} %param.8) | copy-start | bytes 6148
  1.3 0.9 %copy-start = (bf16[512,256]{1,0:T(8,128)(2,1)S(1)}, bf16[512,256]{1,0:T(8,128)(2,1)}, u32[]{:S(2)}) copy-start(bf16[512,256]{1,0:T(8,128)(2,1)} %tgt.1) | copy-start | bytes 786436
  2.3 0.8 %copy-start.1 = (bf16[64,256]{1,0:T(8,128)(2,1)S(1)}, bf16[64,256]{1,0:T(8,128)(2,1)}, u32[]{:S(2)}) copy-start(bf16[64,256]{1,0:T(8,128)(2,1)} %src.1) | copy-start | bytes 98308
  3.0 0.7 %copy-start.2 = (f32[2048]{0:T(1024)S(1)}, f32[2048]{0:T(1024)}, u32[]{:S(2)}) copy-start(f32[2048]{0:T(1024)} %param.7) | copy-start | bytes 24580

commit v3 on v2

v3 whole, which is shorter than its diff:
```python
import functools
import jax
import jax.numpy as jnp
from jax import lax
from jax.experimental import pallas as pl
from jax.experimental.pallas import tpu as pltpu
from jax.sharding import PartitionSpec as P

score_scale = 0.1875
F32 = jnp.float32
BF16 = jnp.bfloat16


def kernel(R, NC, ND, src_h, tgt_h, dual_h, weight_h, match_h, gs_out, gt_out,
           tgt, dual_all, weight, match_in, S, T2, dual, dual2, wm, wm_all, wm_g, dcol, e_buf, m_buf, lam,
           dbuf, ps, px, zs, zr, partf, gt_send, gt_recv,
           s_in, s_pair, r_pair, s_z, r_z, s_x, r_x, s_wm, r_wm, s_l, r_l, s_p, r_p, s_zp, r_zp):
    G = (NC // 2) * ND
    N = R * G
    n, D = src_h.shape
    own = tgt_h.shape[0]
    C = R * n
    row = lax.axis_index("row")
    col = lax.axis_index("col")
    dep = lax.axis_index("depth")
    par = lax.rem(col, 2)
    grp = (col // 2) * ND + dep
    me = grp * R + row
    sib_col = col + 1 - 2 * par
    order = sorted(range(G), key=lambda g: abs(2 * g - G + 1))
    MESH = pl.DeviceIdType.MESH

    def dev(r, c, d):
        return {"row": r, "col": c, "depth": d}

    sib = dev(row, sib_col, dep)

    def xpeer(k):
        r = lax.rem(row + k, R)
        return r, dev(r, col, dep)

    def zdev(g):
        return dev(row, (g // ND) * 2 + par, g % ND)

    def peer(k):
        i = lax.rem(me + k, N)
        g = i // R
        return dev(lax.rem(i, R), (g // ND) * 2 + par, lax.rem(g, ND))

    def rcopy(a, b, ss, rs, to):
        return pltpu.make_async_remote_copy(src_ref=a, dst_ref=b, send_sem=ss, recv_sem=rs,
                                            device_id=to, device_id_type=MESH)

    def each_peer(fn):
        if N <= 32:
            for k in range(1, N):
                fn(k)
        else:
            lax.fori_loop(1, N, lambda k, c: (fn(k), c)[1], 0)

    barrier = pltpu.get_barrier_semaphore()
    pl.semaphore_signal(barrier, inc=1, device_id=sib, device_id_type=MESH)
    each_peer(lambda k: pl.semaphore_signal(barrier, inc=1, device_id=peer(k), device_id_type=MESH))
    loads = [pltpu.make_async_copy(a, b, s_in.at[i]) for i, (a, b) in enumerate((
        (src_h, S.at[grp, row]), (tgt_h, tgt), (dual_h, dual_all), (weight_h, weight), (match_h, match_in)))]
    for c in loads:
        c.start()
    for c in loads:
        c.wait()

    dual[...] = dual_all[:, pl.ds(pl.multiple_of(row * own, own), own)]
    for i, vec in ((0, weight[...]), (1, match_in[...].astype(F32))):
        span = ND * n
        parts = [jnp.where(par == 0, vec[:, 2 * c * span:(2 * c + 1) * span],
                           vec[:, (2 * c + 1) * span:(2 * c + 2) * span]) for c in range(NC // 2)]
        wm[i:i + 1, :] = parts[0] if len(parts) == 1 else jnp.concatenate(parts, axis=1)
    wm_all[row] = wm[...]
    dcol[0:own, :] = jnp.transpose(jnp.broadcast_to(dual[...], (128, own)))
    pl.semaphore_wait(barrier, N)

    sends = []

    def go(c):
        c.start()
        sends.append(c)

    mine_s = S.at[grp, row]

    def z_send(g):
        return rcopy(mine_s, S.at[grp, row], s_z.at[g], r_z.at[grp], zdev(g))

    def x_send(g, j):
        return rcopy(S.at[g, row], S.at[g, row], s_x.at[j, g], r_x.at[row, g], xpeer(j)[1])

    for g in order:
        @pl.when(grp != g)
        def _(g=g):
            z_send(g).start()
    for j in range(1, R):
        x_send(grp, j).start()
    go(rcopy(tgt, T2, s_pair.at[0], r_pair.at[0], sib))
    go(rcopy(dual, dual2, s_pair.at[1], r_pair.at[1], sib))
    for g in order:
        @pl.when(grp != g)
        def _(g=g):
            rcopy(mine_s, S.at[g, row], s_z.at[g], r_z.at[g], zdev(g)).wait_recv()
            for j in range(1, R):
                x_send(g, j).start()
    for k in range(1, R):
        go(rcopy(wm, wm_all.at[row], s_wm.at[k], r_wm.at[row], xpeer(k)[1]))
    rcopy(dual, dual2, s_pair.at[1], r_pair.at[1], sib).wait_recv()
    dcol[own:2 * own, :] = jnp.transpose(jnp.broadcast_to(dual2[...], (128, own)))
    rcopy(tgt, T2, s_pair.at[0], r_pair.at[0], sib).wait_recv()

    lane_rep = C // 128

    def scores_chunk(g):
        rows = S[g].reshape(C, D)
        tops = []
        for h, t in ((0, tgt), (1, T2)):
            p = lax.dot_general(t[...], rows, (((1,), (1,)), ((), ())), preferred_element_type=F32)
            dc = dcol[h * own:(h + 1) * own, :]
            s = score_scale * p + jnp.concatenate([dc] * lane_rep, axis=1)
            e_buf[g, h * own:(h + 1) * own, :] = s
            tops.append(jnp.max(s, axis=0, keepdims=True))
        top = jnp.maximum(tops[0], tops[1])
        m_buf[g] = top
        e = jnp.exp(e_buf[g] - top)
        e_buf[g] = e
        lam[g, me] = top + jnp.log(jnp.sum(e, axis=0, keepdims=True))

    def gather_wait(g):
        for j in range(1, R):
            r, to = xpeer(j)
            rcopy(mine_s, S.at[g, r], s_x.at[0, 0], r_x.at[r, g], to).wait_recv()

    for g in order:
        gather_wait(g)
        scores_chunk(g)
        each_peer(lambda k: rcopy(lam.at[g, me], lam.at[g, me], s_l.at[g], r_l.at[g], peer(k)).start())

    for k in range(1, R):
        r, to = xpeer(k)
        rcopy(wm, wm_all.at[r], s_wm.at[k], r_wm.at[r], to).wait_recv()
    for g in range(G):
        for i in range(2):
            wm_g[g, i:i + 1, :] = jnp.concatenate(
                [wm_all[r, i:i + 1, g * n:(g + 1) * n] for r in range(R)], axis=1)

    first = [((c * ND + dep) * R + row) * own for c in (col, sib_col)]

    def lam_all(g):
        every = lam.at[g, pl.ds(0, N - 1)]
        return rcopy(every, every, s_l.at[g], r_l.at[g], sib)

    def delta_chunk(g):
        lam_all(g).wait_recv()
        parts = lam[g]
        peak = jnp.max(parts, axis=0)
        log_total = peak + jnp.log(jnp.sum(jnp.exp(parts - peak[None]), axis=0))
        w = wm_g[g, 0:1, :]
        match = wm_g[g, 1:2, :].astype(jnp.int32)
        scale = w * jnp.exp(m_buf[g] - log_total)
        part = None
        for h, t in ((0, tgt), (1, T2)):
            ids = lax.broadcasted_iota(jnp.int32, (own, C), 0)
            hit = jnp.where(ids == match - first[h], w, 0.0)
            d = (scale * e_buf[g, h * own:(h + 1) * own, :] - hit).astype(BF16)
            dbuf[g, h * own:(h + 1) * own, :] = d
            q = lax.dot_general(d, t[...], (((0,), (0,)), ((), ())), preferred_element_type=F32)
            part = q if part is None else part + q
        return part

    for g in order:
        part = delta_chunk(g).reshape(R, n, D)
        partf[g] = part
        ps[g] = part.astype(BF16)
        for k in range(1, R):
            r, to = xpeer(k)
            go(rcopy(ps.at[g, r], px.at[g, row], s_p.at[k, g], r_p.at[row, g], to))

    def gt_half(h):
        acc = None
        for g in range(G):
            q = jnp.dot(dbuf[g, h * own:(h + 1) * own, :], S[g].reshape(C, D), preferred_element_type=F32)
            acc = q if acc is None else acc + q
        return acc

    gt_send[...] = gt_half(1)
    go(rcopy(gt_send, gt_recv, s_pair.at[2], r_pair.at[2], sib))

    def stage_sum(g):
        acc = partf[g, row]
        for k in range(1, R):
            acc = acc + px[g, lax.rem(row + k, R)].astype(F32)
        return acc

    def zp_send(g):
        return rcopy(zs.at[g], zr.at[grp], s_zp.at[g], r_zp.at[grp], zdev(g))

    for g in order:
        for k in range(1, R):
            r, to = xpeer(k)
            rcopy(ps.at[g, r], px.at[g, r], s_p.at[k, 0], r_p.at[r, g], to).wait_recv()
        zs[g] = stage_sum(g).astype(BF16)

        @pl.when(grp != g)
        def _(g=g):
            zp_send(g).start()

    gt_out[...] = gt_half(0)
    rcopy(gt_send, gt_recv, s_pair.at[2], r_pair.at[2], sib).wait_recv()
    gt_out[...] = score_scale * (gt_out[...] + gt_recv[...])

    gs_out[...] = stage_sum(grp)
    for g in order:
        @pl.when(grp != g)
        def _(g=g):
            rcopy(zs.at[g], zr.at[g], s_zp.at[g], r_zp.at[g], zdev(g)).wait_recv()
            gs_out[...] = gs_out[...] + zr[g].astype(F32)
    gs_out[...] = score_scale * gs_out[...]

    for c in sends:
        c.wait_send()
    for g in range(G):
        lam_all(g).wait_send()
        for j in range(1, R):
            x_send(g, j).wait_send()

        @pl.when(grp != g)
        def _(g=g):
            z_send(g).wait_send()
            zp_send(g).wait_send()


def per_device(R, NC, ND, source_desc, target_desc, target_dual, row_weight, matches):
    n, D = source_desc.shape
    own = target_desc.shape[0]
    G = (NC // 2) * ND
    C = R * n
    vm = pl.BlockSpec(memory_space=pltpu.VMEM)
    dma = pltpu.SemaphoreType.DMA
    return pl.pallas_call(
        functools.partial(kernel, R, NC, ND),
        out_shape=(jax.ShapeDtypeStruct((n, D), F32), jax.ShapeDtypeStruct((own, D), F32)),
        in_specs=[pl.BlockSpec(memory_space=pltpu.HBM)] * 5,
        out_specs=(vm, vm),
        scratch_shapes=[
            pltpu.VMEM((own, D), BF16),
            pltpu.VMEM((1, target_dual.shape[0]), F32),
            pltpu.VMEM((1, row_weight.shape[0]), F32),
            pltpu.VMEM((1, row_weight.shape[0]), jnp.int32),
            pltpu.VMEM((G, R, n, D), BF16),
            pltpu.VMEM((own, D), BF16),
            pltpu.VMEM((1, own), F32),
            pltpu.VMEM((1, own), F32),
            pltpu.VMEM((2, G * n), F32),
            pltpu.VMEM((R, 2, G * n), F32),
            pltpu.VMEM((G, 2, C), F32),
            pltpu.VMEM((2 * own, 128), F32),
            pltpu.VMEM((G, 2 * own, C), F32),
            pltpu.VMEM((G, 1, C), F32),
            pltpu.VMEM((G, R * G, 1, C), F32),
            pltpu.VMEM((G, 2 * own, C), BF16),
            pltpu.VMEM((G, R, n, D), BF16),
            pltpu.VMEM((G, R, n, D), BF16),
            pltpu.VMEM((G, n, D), BF16),
            pltpu.VMEM((G, n, D), BF16),
            pltpu.VMEM((G, R, n, D), F32),
            pltpu.VMEM((own, D), F32),
            pltpu.VMEM((own, D), F32),
            dma((5,)),
            dma((3,)), dma((3,)),
            dma((G,)), dma((G,)),
            dma((R, G)), dma((R, G)),
            dma((R,)), dma((R,)),
            dma((G,)), dma((G,)),
            dma((R, G)), dma((R, G)),
            dma((G,)), dma((G,)),
        ],
        compiler_params=pltpu.CompilerParams(collective_id=0, has_side_effects=True,
                                             vmem_limit_bytes=32 * 1024 * 1024),
    )(source_desc, target_desc, target_dual[None, :], row_weight[None, :], matches[None, :])


def solution(mesh):
    R, NC, ND = mesh.shape["row"], mesh.shape["col"], mesh.shape["depth"]
    return jax.shard_map(
        functools.partial(per_device, R, NC, ND),
        mesh=mesh,
        in_specs=(
            P(("row", "col", "depth"), None),
            P(("col", "depth", "row"), None),
            P(("col", "depth")),
            P("row"),
            P("row"),
        ),
        out_specs=(P(("row", "col", "depth"), None), P(("col", "depth", "row"), None)),
        check_vma=False,
    )
```

time: 38.7 us -> 35.6 us (0.920)
  Pallas kernels: 33.3 us -> 30.2 us
    pallas_call x1, Pallas kernels: 33.3 us -> 30.2 us  [per_device(): pl.pallas_call(functools.partial(kernel, R, NC, ND), out_shape=(jax.Shape...]
where the time goes in v3:
time: 35.6 us; the launch traced here: 35.3 us
  Pallas kernels  30.2 us (85%)
  local copies, waits for them, and re-layouts  4.51 us (13%)
  between operations  0.66 us (2%)
    pallas_call x1, Pallas kernels, per_device(): pl.pallas_call(functools.partial(kernel, R, NC, ND), out_shape=(jax.Shape...  30.2 us
    unnamed x12, local copies, waits for them, and re-layouts  4.51 us

profile of v3, /device:TPU:0, one launch (start us, length us, event | category | flops | bytes accessed | tf_op | source)
XLA Modules:
  0.0 35.3 jit_solution(2587957491011310192)
XLA Ops:
  0.6 0.0 copy-start.4
  0.6 0.0 copy-start.3
  0.7 0.7 %copy-done.4 = s32[512]{0:T(512)S(1)} copy-done((s32[512]{0:T(512)S(1)}, s32[512]{0:T(512)}, u32[]{:S(2)}) %copy-start.4) | copy-done | bytes 2072
  1.3 0.0 copy-done.3
  1.3 0.0 copy-start
  1.3 0.9 %copy-done = bf16[512,256]{1,0:T(8,128)(2,1)S(1)} copy-done((bf16[512,256]{1,0:T(8,128)(2,1)S(1)}, bf16[512,256]{1,0:T(8,128)(2,1)}, u32[]{:S(2)}) %copy-start) | copy-done | bytes 262168
  2.3 0.0 copy-start.1
  2.3 0.8 %copy-done.1 = bf16[64,256]{1,0:T(8,128)(2,1)S(1)} copy-done((bf16[64,256]{1,0:T(8,128)(2,1)S(1)}, bf16[64,256]{1,0:T(8,128)(2,1)}, u32[]{:S(2)}) %copy-start.1) | copy-done | bytes 32792
  3.0 0.0 copy-start.2
  3.0 0.7 %copy-done.2 = f32[2048]{0:T(1024)S(1)} copy-done((f32[2048]{0:T(1024)S(1)}, f32[2048]{0:T(1024)}, u32[]{:S(2)}) %copy-start.2) | copy-done | bytes 8216
  3.7 30.2 %shard_map.68 = (f32[64,256]{1,0:T(8,128)S(1)}, f32[512,256]{1,0:T(8,128)S(1)}) custom-call(bf16[64,256]{1,0:T(8,128)(2,1)S(1)} %copy-done.1, bf16[512,256]{1,0:T(8,128)(2,1)S(1)} %copy-done, f32[1,2048]{1,0:T(1,128)S(1)} %bitcast.3, f32[1,512]{1,0:T(1,128)S(1)} %bitcast.4, s32[1,512]{1,0:T(1,128)S(1)} %bitcast.5), custom_call_target="tpu_custom_call" | custom-call | tf_op jit(solution)/shard_map/pallas_call | solution.py:243
  33.9 0.6 %copy.9 = f32[64,256]{1,0:T(8,128)} copy(f32[64,256]{1,0:T(8,128)S(1)} %get-tuple-element.4) | data formatting | bytes 131072
  34.5 0.8 %copy.10 = f32[512,256]{1,0:T(8,128)} copy(f32[512,256]{1,0:T(8,128)S(1)} %get-tuple-element.5) | data formatting | bytes 1048576
Async XLA Ops:
  0.6 0.7 %copy-start.4 = (s32[512]{0:T(512)S(1)}, s32[512]{0:T(512)}, u32[]{:S(2)}) copy-start(s32[512]{0:T(512)} %param.9) | copy-start | bytes 6148
  0.6 0.7 %copy-start.3 = (f32[512]{0:T(512)S(1)}, f32[512]{0:T(512)}, u32[]{:S(2)}) copy-start(f32[512]{0:T(512)} %param.8) | copy-start | bytes 6148
  1.3 0.9 %copy-start = (bf16[512,256]{1,0:T(8,128)(2,1)S(1)}, bf16[512,256]{1,0:T(8,128)(2,1)}, u32[]{:S(2)}) copy-start(bf16[512,256]{1,0:T(8,128)(2,1)} %tgt_h.1) | copy-start | bytes 786436
  2.3 0.8 %copy-start.1 = (bf16[64,256]{1,0:T(8,128)(2,1)S(1)}, bf16[64,256]{1,0:T(8,128)(2,1)}, u32[]{:S(2)}) copy-start(bf16[64,256]{1,0:T(8,128)(2,1)} %src_h.1) | copy-start | bytes 98308
  3.0 0.7 %copy-start.2 = (f32[2048]{0:T(1024)S(1)}, f32[2048]{0:T(1024)}, u32[]{:S(2)}) copy-start(f32[2048]{0:T(1024)} %param.7) | copy-start | bytes 24580

commit v4 on v3

--- a/solution.py
+++ b/solution.py
@@ -14,7 +14,7 @@
 def kernel(R, NC, ND, src_h, tgt_h, dual_h, weight_h, match_h, gs_out, gt_out,
            tgt, dual_all, weight, match_in, S, T2, dual, dual2, wm, wm_all, wm_g, dcol, e_buf, m_buf, lam,
            dbuf, ps, px, zs, zr, partf, gt_send, gt_recv,
-           s_in, s_pair, r_pair, s_z, r_z, s_x, r_x, s_wm, r_wm, s_l, r_l, s_p, r_p, s_zp, r_zp):
+           s_in, s_pair, r_pair, s_z, r_z, s_x, r_x, s_wm, r_wm, s_l, r_l, s_p, r_p, s_zp, r_zp, line_in):
     G = (NC // 2) * ND
     N = R * G
     n, D = src_h.shape
@@ -36,8 +36,7 @@
     sib = dev(row, sib_col, dep)
 
     def xpeer(k):
-        r = lax.rem(row + k, R)
-        return r, dev(r, col, dep)
+        return ring[k], dev(ring[k], col, dep)
 
     def zdev(g):
         return dev(row, (g // ND) * 2 + par, g % ND)
@@ -51,21 +50,33 @@
         return pltpu.make_async_remote_copy(src_ref=a, dst_ref=b, send_sem=ss, recv_sem=rs,
                                             device_id=to, device_id_type=MESH)
 
+    ring = [lax.rem(row + j, R) for j in range(R)]
+
     def each_peer(fn):
         if N <= 32:
-            for k in range(1, N):
-                fn(k)
+            for g in range(G):
+                for j in range(R - 1, 0, -1):
+                    fn(dev(ring[j], (g // ND) * 2 + par, g % ND))
+
+                @pl.when(grp != g)
+                def _(g=g):
+                    fn(zdev(g))
         else:
-            lax.fori_loop(1, N, lambda k, c: (fn(k), c)[1], 0)
+            lax.fori_loop(1, N, lambda k, c: (fn(peer(k)), c)[1], 0)
 
     barrier = pltpu.get_barrier_semaphore()
     pl.semaphore_signal(barrier, inc=1, device_id=sib, device_id_type=MESH)
-    each_peer(lambda k: pl.semaphore_signal(barrier, inc=1, device_id=peer(k), device_id_type=MESH))
+    for j in range(1, R):
+        pl.semaphore_signal(barrier, inc=1, device_id=xpeer(j)[1], device_id_type=MESH)
+    for g in range(G):
+        @pl.when(grp != g)
+        def _(g=g):
+            pl.semaphore_signal(barrier, inc=1, device_id=zdev(g), device_id_type=MESH)
     loads = [pltpu.make_async_copy(a, b, s_in.at[i]) for i, (a, b) in enumerate((
         (src_h, S.at[grp, row]), (tgt_h, tgt), (dual_h, dual_all), (weight_h, weight), (match_h, match_in)))]
     for c in loads:
         c.start()
-    for c in loads:
+    for c in loads[2:]:
         c.wait()
 
     dual[...] = dual_all[:, pl.ds(pl.multiple_of(row * own, own), own)]
@@ -76,7 +87,9 @@
         wm[i:i + 1, :] = parts[0] if len(parts) == 1 else jnp.concatenate(parts, axis=1)
     wm_all[row] = wm[...]
     dcol[0:own, :] = jnp.transpose(jnp.broadcast_to(dual[...], (128, own)))
-    pl.semaphore_wait(barrier, N)
+    for c in loads[:2]:
+        c.wait()
+    pl.semaphore_wait(barrier, R + G - 1)
 
     sends = []
 
@@ -107,6 +120,7 @@
             for j in range(1, R):
                 x_send(g, j).start()
     for k in range(1, R):
+        pl.semaphore_signal(line_in, inc=1, device_id=xpeer(k)[1], device_id_type=MESH)
         go(rcopy(wm, wm_all.at[row], s_wm.at[k], r_wm.at[row], xpeer(k)[1]))
     rcopy(dual, dual2, s_pair.at[1], r_pair.at[1], sib).wait_recv()
     dcol[own:2 * own, :] = jnp.transpose(jnp.broadcast_to(dual2[...], (128, own)))
@@ -134,10 +148,12 @@
             r, to = xpeer(j)
             rcopy(mine_s, S.at[g, r], s_x.at[0, 0], r_x.at[r, g], to).wait_recv()
 
-    for g in order:
+    for i, g in enumerate(order):
         gather_wait(g)
         scores_chunk(g)
-        each_peer(lambda k: rcopy(lam.at[g, me], lam.at[g, me], s_l.at[g], r_l.at[g], peer(k)).start())
+        if i == 0:
+            pl.semaphore_wait(line_in, R - 1)
+        each_peer(lambda to: rcopy(lam.at[g, me], lam.at[g, me], s_l.at[g], r_l.at[g], to).start())
 
     for k in range(1, R):
         r, to = xpeer(k)
@@ -192,7 +208,7 @@
     def stage_sum(g):
         acc = partf[g, row]
         for k in range(1, R):
-            acc = acc + px[g, lax.rem(row + k, R)].astype(F32)
+            acc = acc + px[g, ring[k]].astype(F32)
         return acc
 
     def zp_send(g):
@@ -277,10 +293,12 @@
             dma((G,)), dma((G,)),
             dma((R, G)), dma((R, G)),
             dma((G,)), dma((G,)),
+            pltpu.SemaphoreType.REGULAR,
         ],
         compiler_params=pltpu.CompilerParams(collective_id=0, has_side_effects=True,
                                              vmem_limit_bytes=32 * 1024 * 1024),
-    )(source_desc, target_desc, target_dual[None, :], row_weight[None, :], matches[None, :])
+    )(*[pltpu.with_memory_space_constraint(a, pltpu.HBM) for a in (
+        source_desc, target_desc, target_dual[None, :], row_weight[None, :], matches[None, :])])
 
 
 def solution(mesh):

time: 35.6 us -> 31.1 us (0.87)
  local copies, waits for them, and re-layouts: 4.51 us -> 1.42 us
  Pallas kernels: 30.2 us -> 28.9 us
    unnamed x12 -> x2, local copies, waits for them, and re-layouts: 4.51 us -> 1.42 us
    pallas_call x1, Pallas kernels: 30.2 us -> 28.9 us  [per_device(): pl.pallas_call(functools.partial(kernel, R, NC, ND), out_shape=(jax.Shape...]
where the time goes in v4:
time: 31.1 us; the launch traced here: 31 us
  Pallas kernels  28.9 us (93%)
  local copies, waits for them, and re-layouts  1.42 us (5%)
  between operations  0.64 us (2%)
    pallas_call x1, Pallas kernels, per_device(): pl.pallas_call(functools.partial(kernel, R, NC, ND), out_shape=(jax.Shape...  28.9 us
    unnamed x2, local copies, waits for them, and re-layouts  1.42 us

profile of v4, /device:TPU:0, one launch (start us, length us, event | category | flops | bytes accessed | tf_op | source)
XLA Modules:
  0.0 31.0 jit_solution(1736311518285904846)
XLA Ops:
  0.6 28.9 %shard_map.68 = (f32[64,256]{1,0:T(8,128)S(1)}, f32[512,256]{1,0:T(8,128)S(1)}) custom-call(bf16[64,256]{1,0:T(8,128)(2,1)} %src_h.1, bf16[512,256]{1,0:T(8,128)(2,1)} %tgt_h.1, f32[1,2048]{1,0:T(1,128)} %bitcast.3, f32[1,512]{1,0:T(1,128)} %bitcast.4, s32[1,512]{1,0:T(1,128)} %bitcast.5), custom_call_target="tpu_custom_call" | custom-call | tf_op jit(solution)/shard_map/pallas_call | solution.py:259
  29.6 0.6 %copy.9 = f32[64,256]{1,0:T(8,128)} copy(f32[64,256]{1,0:T(8,128)S(1)} %get-tuple-element.4) | data formatting | bytes 131072
  30.2 0.8 %copy.10 = f32[512,256]{1,0:T(8,128)} copy(f32[512,256]{1,0:T(8,128)S(1)} %get-tuple-element.5) | data formatting | bytes 1048576

commit v5 on v4

--- a/solution.py
+++ b/solution.py
@@ -249,6 +249,14 @@
             zp_send(g).wait_send()
 
 
+def flush(gs, gt, gs_out, gt_out, sem):
+    copies = [pltpu.make_async_copy(gt, gt_out, sem.at[0]), pltpu.make_async_copy(gs, gs_out, sem.at[1])]
+    for c in copies:
+        c.start()
+    for c in copies:
+        c.wait()
+
+
 def per_device(R, NC, ND, source_desc, target_desc, target_dual, row_weight, matches):
     n, D = source_desc.shape
     own = target_desc.shape[0]
@@ -256,7 +264,7 @@
     C = R * n
     vm = pl.BlockSpec(memory_space=pltpu.VMEM)
     dma = pltpu.SemaphoreType.DMA
-    return pl.pallas_call(
+    outs = pl.pallas_call(
         functools.partial(kernel, R, NC, ND),
         out_shape=(jax.ShapeDtypeStruct((n, D), F32), jax.ShapeDtypeStruct((own, D), F32)),
         in_specs=[pl.BlockSpec(memory_space=pltpu.HBM)] * 5,
@@ -299,6 +307,15 @@
                                              vmem_limit_bytes=32 * 1024 * 1024),
     )(*[pltpu.with_memory_space_constraint(a, pltpu.HBM) for a in (
         source_desc, target_desc, target_dual[None, :], row_weight[None, :], matches[None, :])])
+    hbm = pl.BlockSpec(memory_space=pltpu.HBM)
+    return pl.pallas_call(
+        flush,
+        out_shape=(jax.ShapeDtypeStruct((n, D), F32), jax.ShapeDtypeStruct((own, D), F32)),
+        in_specs=[vm, vm],
+        out_specs=(hbm, hbm),
+        scratch_shapes=[dma((2,))],
+        compiler_params=pltpu.CompilerParams(vmem_limit_bytes=8 * 1024 * 1024),
+    )(*outs)
 
 
 def solution(mesh):

time: 31.1 us -> 30.5 us (0.981)
  local copies, waits for them, and re-layouts: 1.42 us -> 0 us
  Pallas kernels: 28.9 us -> 29.7 us
    unnamed x2 -> x0, local copies, waits for them, and re-layouts: 1.42 us -> none
    pallas_call x0 -> x1, Pallas kernels: none -> 0.82 us  [per_device(): pl.pallas_call(flush, out_shape=(jax.ShapeDtypeStruct((n, D), F32), jax.S...]
where the time goes in v5:
time: 30.5 us; the launch traced here: 30.4 us
  Pallas kernels  29.7 us (97%)
  between operations  0.64 us (2%)
    pallas_call x1, Pallas kernels, per_device(): pl.pallas_call(functools.partial(kernel, R, NC, ND), out_shape=(jax.Shape...  28.9 us
    pallas_call x1, Pallas kernels, per_device(): pl.pallas_call(flush, out_shape=(jax.ShapeDtypeStruct((n, D), F32), jax.S...  0.82 us

profile of v5, /device:TPU:0, one launch (start us, length us, event | category | flops | bytes accessed | tf_op | source)
XLA Modules:
  0.0 30.4 jit_solution(7028827164422749407)
XLA Ops:
  0.6 28.9 %shard_map.68 = (f32[64,256]{1,0:T(8,128)S(1)}, f32[512,256]{1,0:T(8,128)S(1)}) custom-call(bf16[64,256]{1,0:T(8,128)(2,1)} %src_h.1, bf16[512,256]{1,0:T(8,128)(2,1)} %tgt_h.1, f32[1,2048]{1,0:T(1,128)} %bitcast.3, f32[1,512]{1,0:T(1,128)} %bitcast.4, s32[1,512]{1,0:T(1,128)} %bitcast.5), custom_call_target="tpu_custom_call" | custom-call | tf_op jit(solution)/shard_map/pallas_call | solution.py:267
  29.6 0.8 %shard_map.69 = (f32[64,256]{1,0:T(8,128)}, f32[512,256]{1,0:T(8,128)}) custom-call(f32[64,256]{1,0:T(8,128)S(1)} %get-tuple-element.4.gs, f32[512,256]{1,0:T(8,128)S(1)} %get-tuple-element.5.gt), custom_call_target="tpu_custom_call" | custom-call | tf_op jit(solution)/shard_map/pallas_call | solution.py:311
